TPU v7x, 256 devices: a whole 4x4x8 slice. The times are simulated.
256 devices in a mesh: row: 16 (over z, core), col: 16 (over x, y).
Axes of the slice: x: 4, y: 4, z: 8, core: 2. Of those that a mesh axis runs over, the one named last changes fastest.
Arguments:
- multipliers: float32 [256, 2, 16, 256], P(('row', 'col')), may hold values from -6 to 6
- residual: float32 [256, 2, 16, 256], P(('row', 'col')), may hold values from -18 to 18
- direction: float32 [256, 2, 16, 256], P(('row', 'col')), may hold values from -6 to 6
- energy_prev: float32 [16], replicated, may hold values from 262144 to 1048576
- hypersingular: bfloat16 [256, 1152, 1152], P(('row', 'col')), may hold values from -1 to 4, as said below
- double_layer: bfloat16 [256, 1152, 1152], P(('row', 'col')), may hold values from -0.1875 to 0.1875
- single_inverse: bfloat16 [256, 1152, 1152], P(('row', 'col')), may hold values from -1 to 4, as said below
- neumann_inverse: bfloat16 [256, 1152, 1152], P(('row', 'col')), may hold values from -1 to 4, as said below
- rigid_modes: float32 [256, 6, 1152], P(('row', 'col')), may hold values from -0.75 to 0.75
- coarse_inverse: float32 [1536, 1536], P(('row', 'col')), may hold values from -0.625 to 0.625
- face_index: int32 [256, 4, 256], P(('row', 'col')), may hold values from 0 to 1151, as said below
Outputs:
- multipliers_next: float32 [256, 2, 16, 256], P(('row', 'col'))
- residual_next: float32 [256, 2, 16, 256], P(('row', 'col'))
- direction_next: float32 [256, 2, 16, 256], P(('row', 'col'))
Inputs may be any that keep to these rules, and one draw needn't show every extreme that they name: For each patch the 1024 entries of face_index are distinct. `hypersingular`: each patch's matrix is symmetric positive definite. `single_inverse`: each patch's matrix is symmetric positive definite. `neumann_inverse`: each patch's matrix is symmetric positive definite.
All inputs are finite; a program needn't handle non-finite values.
Results may differ from a plain program's by a relative error of at most 0.0015.
Values sent between devices are 32-bit elements; how exact they have to be, the bound alone decides.
No kernel may reach another device: no remote copies, remote signals or barrier semaphores. Data moves between devices by JAX's collectives and lax.ppermute only.
A program may use at most 64 MiB of HBM per device.

v0:
```python
import jax
import jax.numpy as jnp
from jax import lax
from jax.sharding import PartitionSpec as P

NB = 1152
highest = lax.Precision.HIGHEST
contract_last = (((1,), (1,)), ((), ()))
contract_first = (((0,), (0,)), ((), ()))


def shifted(block, axis, distance):
    devices = range(lax.axis_size(axis))
    route = [((i - distance) % len(devices), i) for i in devices]
    return lax.ppermute(block, axis, route)


def spread_faces(values, face_where):
    from_left = shifted(values[0], "col", 1)
    from_below = shifted(values[1], "row", 1)
    pieces = jnp.concatenate([values[0], values[1], -from_left, -from_below], axis=1)
    return jnp.zeros((values.shape[1], NB), jnp.float32).at[:, face_where].set(pieces)


def jump_faces(vectors, face_where):
    face_width = face_where.shape[0] // 4
    picked = jnp.take(vectors, face_where, axis=1)
    from_right = shifted(picked[:, 2 * face_width : 3 * face_width], "col", -1)
    from_above = shifted(picked[:, 3 * face_width :], "row", -1)
    return jnp.stack(
        [picked[:, :face_width] - from_right, picked[:, face_width : 2 * face_width] - from_above]
    )


def project(values, face_where, rigid_local, coarse_rows):
    spread = spread_faces(values, face_where)
    partial_value = lax.dot_general(rigid_local, spread, contract_last, precision=highest)
    coarse_coef = jnp.dot(
        coarse_rows,
        lax.all_gather(partial_value, ("row", "col"), axis=0, tiled=True),
        precision=highest,
    )
    modes_back = lax.dot_general(coarse_coef, rigid_local, contract_first, precision=highest)
    correction = jump_faces(modes_back, face_where)
    return values - correction


def on_device(
    multipliers,
    residual,
    direction,
    energy_prev,
    hypersingular,
    double_layer,
    single_inverse,
    neumann_inverse,
    rigid_modes,
    coarse_inverse,
    face_index,
):
    face_where = face_index[0].reshape(-1)
    rigid_local = rigid_modes[0]
    hyper_local = hypersingular[0]
    double_local = double_layer[0]
    single_local = single_inverse[0]
    neumann_local = neumann_inverse[0]
    multipliers_now = multipliers[0]
    residual_now = residual[0]
    direction_now = direction[0]
    cases = residual_now.shape[1]
    projected = project(residual_now, face_where, rigid_local, coarse_inverse)
    rounded = spread_faces(projected, face_where).astype(jnp.bfloat16)
    lifted = (
        0.5 * rounded.astype(jnp.float32)
        + jnp.dot(rounded, double_local, preferred_element_type=jnp.float32)
    ).astype(jnp.bfloat16)
    weighed = jnp.dot(lifted, single_local, preferred_element_type=jnp.float32).astype(jnp.bfloat16)
    applied = (
        jnp.dot(rounded, hyper_local, preferred_element_type=jnp.float32)
        + 0.5 * weighed.astype(jnp.float32)
        + lax.dot_general(weighed, double_local, contract_last, preferred_element_type=jnp.float32)
    )
    energy_local = jnp.sum(rounded.astype(jnp.float32) * applied, axis=1)
    searched = project(jump_faces(applied, face_where), face_where, rigid_local, coarse_inverse)
    paired = spread_faces(jnp.concatenate([searched, direction_now], axis=1), face_where).astype(
        jnp.bfloat16
    )
    paired_applied = jnp.dot(paired, neumann_local, preferred_element_type=jnp.float32)
    paired_new = paired[:cases].astype(jnp.float32)
    paired_old = paired[cases:].astype(jnp.float32)
    applied_new = paired_applied[:cases]
    applied_old = paired_applied[cases:]
    energy = lax.psum(energy_local, ("row", "col"))
    step_ratio = energy / energy_prev
    spread_dir = paired_new + step_ratio[:, None] * paired_old
    applied_dir = applied_new + step_ratio[:, None] * applied_old
    curvature = lax.psum(jnp.sum(spread_dir * applied_dir, axis=1), ("row", "col"))
    step_size = energy / curvature
    direction_now = searched + step_ratio[None, :, None] * direction_now
    multipliers_now = multipliers_now + step_size[None, :, None] * direction_now
    corrected = project(
        jump_faces(applied_dir, face_where), face_where, rigid_local, coarse_inverse
    )
    residual_now = residual_now - step_size[None, :, None] * corrected
    return (multipliers_now[None], residual_now[None], direction_now[None])


def solution(mesh):
    return jax.shard_map(
        on_device,
        mesh=mesh,
        in_specs=(
            P(("row", "col"), None, None, None),
            P(("row", "col"), None, None, None),
            P(("row", "col"), None, None, None),
            P(),
            P(("row", "col"), None, None),
            P(("row", "col"), None, None),
            P(("row", "col"), None, None),
            P(("row", "col"), None, None),
            P(("row", "col"), None, None),
            P(("row", "col"), None),
            P(("row", "col"), None, None),
        ),
        out_specs=(
            P(("row", "col"), None, None, None),
            P(("row", "col"), None, None, None),
            P(("row", "col"), None, None, None),
        ),
        check_vma=False,
    )
```

profile of v0, /device:TPU:1, one launch (start us, length us, event | category | flops | bytes accessed | tf_op | source)
XLA Modules:
  0.0 625.8 jit_solution(15641244841059424459)
XLA Ops:
  3.7 2.5 collective-permute-start.1
  9.5 3.6 scatter_custom_fusion
  14.3 111.3 %all-gather = f32[256,6,16]{2,1,0:T(8,128)} all-gather(f32[1,6,16]{2,1,0:T(8,128)S(1)} %convolution_bitcast_fusion.2), channel_id=1, replica_groups=mesh['row'=16,'col'=16] {'row','col'}, dimensions={0}, use_global_device_ids=true | all-gather | bytes 98688 | tf_op jit(solution)/shard_map/all_gather | solution.py:40
  128.6 4.0 gather_fusion
  133.9 2.5 collective-permute-start.2
  145.0 6.5 %collective-permute-done.4 = f32[16,256]{1,0:T(8,128)S(1)} collective-permute-done((f32[16,256]{1,0:T(8,128)S(1)}, f32[16,256]{1,0:T(8,128)S(1)}, u32[]{:S(2)}, u32[]{:S(2)}) %collective-permute-start.4) | collective-permute-done | bytes 16416 | tf_op jit(solution)/shard_map/ppermute | solution.py:15
  152.5 3.6 scatter_custom_fusion.1
  156.3 2.6 fusion.22
  163.4 4.0 gather_fusion.1
  171.6 3.6 collective-permute-start.7
  176.1 5.6 collective-permute-done.8
  182.8 3.6 scatter_custom_fusion.2
  186.8 107.6 %all-gather.1 = f32[256,6,16]{2,1,0:T(8,128)} all-gather(f32[1,6,16]{2,1,0:T(8,128)S(1)} %convolution_bitcast_fusion.1), channel_id=1, replica_groups=mesh['row'=16,'col'=16] {'row','col'}, dimensions={0}, use_global_device_ids=true | all-gather | bytes 98688 | tf_op jit(solution)/shard_map/all_gather | solution.py:40
  297.4 4.0 gather_fusion.2
  302.7 2.5 collective-permute-start.10
  310.6 79.8 %psum.14 = f32[16]{0:T(128)S(1)} all-reduce(f32[16]{0:T(128)} %get-tuple-element.37), channel_id=1, replica_groups=mesh['row'=16,'col'=16] {'row','col'}, use_global_device_ids=true, to_apply=%region_3.5 | all-reduce | flops 16 | bytes 128 | tf_op jit(solution)/shard_map/psum | solution.py:93
  392.7 3.6 scatter_custom_fusion.3
  399.8 4.0 gather_fusion.3
  410.9 4.5 collective-permute-done.16
  416.5 3.6 scatter_custom_fusion.4
  420.6 108.0 %all-gather.2 = f32[256,6,16]{2,1,0:T(8,128)} all-gather(f32[1,6,16]{2,1,0:T(8,128)S(1)} %convolution_bitcast_fusion), channel_id=1, replica_groups=mesh['row'=16,'col'=16] {'row','col'}, dimensions={0}, use_global_device_ids=true | all-gather | bytes 98688 | tf_op jit(solution)/shard_map/all_gather | solution.py:40
  531.5 4.0 gather_fusion.4
  536.9 2.4 collective-permute-start.18
  546.2 76.4 %psum.15 = f32[16]{0:T(128)S(1)} all-reduce(f32[16]{0:T(128)} %get-tuple-element.12), channel_id=1, replica_groups=mesh['row'=16,'col'=16] {'row','col'}, use_global_device_ids=true, to_apply=%region_7.9 | all-reduce | flops 16 | bytes 128 | tf_op jit(solution)/shard_map/psum | solution.py:97
  (158 shorter events, 70.6 us)
Async XLA Ops:
  0.6 155.6 %copy-start = (bf16[1,1152,1152]{2,1,0:T(8,128)(2,1)S(1)}, bf16[1,1152,1152]{2,1,0:T(8,128)(2,1)}, u32[]{:S(2)}) copy-start(bf16[1,1152,1152]{2,1,0:T(8,128)(2,1)} %param.18) | copy-start | bytes 7962628
  0.6 126.3 %copy-start.4 = (f32[6,1536]{1,0:T(8,128)S(1)}, f32[6,1536]{1,0:T(8,128)}, u32[]{:S(2)}) copy-start(f32[6,1536]{1,0:T(8,128)} %param.22) | copy-start | bytes 110596
  1.6 6.9 %collective-permute-start = (f32[16,256]{1,0:T(8,128)S(1)}, f32[16,256]{1,0:T(8,128)S(1)}, u32[]{:S(2)}, u32[]{:S(2)}) collective-permute-start(f32[16,256]{1,0:T(8,128)S(1)} %get-tuple-element.34), channel_id=1, source_target_pairs={{15,0},{0,1},{1,2},{2,3},{3,4},{4,5},{5,6},{6,7},{7,8},{8,9},{9,10... | collective-permute-start | bytes 49160 | tf_op jit(solution)/shard_map/ppermute | solution.py:15
  3.7 4.8 collective-permute-start.1
  8.5 119.0 %copy-start.2 = (f32[1,6,1152]{2,0,1:T(1,128)S(1)}, f32[1,6,1152]{2,0,1:T(1,128)}, u32[]{:S(2)}) copy-start(f32[1,6,1152]{2,0,1:T(1,128)} %param.21) | copy-start | bytes 82948
  133.9 4.7 collective-permute-start.2
  139.3 4.6 collective-permute-start.3
  144.7 6.7 %collective-permute-start.4 = (f32[16,256]{1,0:T(8,128)S(1)}, f32[16,256]{1,0:T(8,128)S(1)}, u32[]{:S(2)}, u32[]{:S(2)}) collective-permute-start(f32[16,256]{1,0:T(8,128)S(1)} %get-tuple-element.32), channel_id=1, source_target_pairs={{15,0},{0,1},{1,2},{2,3},{3,4},{4,5},{5,6},{6,7},{7,8},{8,9},{9,10... | collective-permute-start | bytes 49160 | tf_op jit(solution)/shard_map/ppermute | solution.py:15
  144.8 6.6 %collective-permute-start.5 = (f32[16,256]{1,0:T(8,128)S(1)}, f32[16,256]{1,0:T(8,128)S(1)}, u32[]{:S(2)}, u32[]{:S(2)}) collective-permute-start(f32[16,256]{1,0:T(8,128)S(1)} %get-tuple-element.33), channel_id=1, source_target_pairs={{240,0},{0,16},{16,32},{32,48},{48,64},{64,80},{80,96},{96,112},{1... | collective-permute-start | bytes 49160 | tf_op jit(solution)/shard_map/ppermute | solution.py:15
  168.7 2.8 collective-permute-start.6
  171.6 4.5 collective-permute-start.7
  175.2 6.5 %collective-permute-start.8 = (f32[16,256]{1,0:T(8,128)S(1)}, f32[16,256]{1,0:T(8,128)S(1)}, u32[]{:S(2)}, u32[]{:S(2)}) collective-permute-start(f32[16,256]{1,0:T(8,128)S(1)} %get-tuple-element.30), channel_id=1, source_target_pairs={{15,0},{0,1},{1,2},{2,3},{3,4},{4,5},{5,6},{6,7},{7,8},{8,9},{9,10... | collective-permute-start | bytes 49160 | tf_op jit(solution)/shard_map/ppermute | solution.py:15
  176.1 5.6 collective-permute-start.9
  302.7 4.4 collective-permute-start.10
  305.2 4.4 collective-permute-start.11
  310.5 81.1 %collective-permute-start.12 = (f32[32,256]{1,0:T(8,128)S(1)}, f32[32,256]{1,0:T(8,128)S(1)}, u32[]{:S(2)}, u32[]{:S(2)}) collective-permute-start(f32[32,256]{1,0:T(8,128)S(1)} %get-tuple-element.28), channel_id=1, source_target_pairs={{15,0},{0,1},{1,2},{2,3},{3,4},{4,5},{5,6},{6,7},{7,8},{8,9},{9,10... | collective-permute-start | bytes 98312 | tf_op jit(solution)/shard_map/ppermute | solution.py:15
  310.6 81.0 %collective-permute-start.13 = (f32[32,256]{1,0:T(8,128)S(1)}, f32[32,256]{1,0:T(8,128)S(1)}, u32[]{:S(2)}, u32[]{:S(2)}) collective-permute-start(f32[32,256]{1,0:T(8,128)S(1)} %get-tuple-element.29), channel_id=1, source_target_pairs={{240,0},{0,16},{16,32},{32,48},{48,64},{64,80},{80,96},{96,112},{1... | collective-permute-start | bytes 98312 | tf_op jit(solution)/shard_map/ppermute | solution.py:15
  405.0 2.7 collective-permute-start.14
  407.7 3.2 collective-permute-start.15
  409.5 5.9 collective-permute-start.16
  410.9 4.6 collective-permute-start.17
  530.4 93.8 %copy-start.8 = (f32[16,256]{1,0:T(8,128)S(1)}, f32[16,256]{1,0:T(8,128)}, u32[]{:S(2)}) copy-start(f32[16,256]{1,0:T(8,128)} %copy-done.6) | copy-start | bytes 49156
  536.9 4.4 collective-permute-start.18
  541.9 81.3 %collective-permute-start.19 = (f32[16,256]{0,1:T(8,128)}, f32[16,256]{0,1:T(8,128)}, u32[]{:S(2)}, u32[]{:S(2)}) collective-permute-start(f32[16,256]{0,1:T(8,128)} %get-tuple-element.19), channel_id=1, source_target_pairs={{16,0},{32,16},{48,32},{64,48},{80,64},{96,80},{112,96},{128,112},... | collective-permute-start | bytes 49160 | tf_op jit(solution)/shard_map/ppermute | solution.py:15
  (18 other events, 417.6 us)
where the time goes:
time: 627 us; the launch traced here: 626 us
  blocking collectives  483 us (77%)
  local copies, waits for them, and re-layouts  58 us (9%)
  waiting for transfers between devices  30.9 us (5%)
  starting transfers between devices  26 us (4%)
  matrix products  14.4 us (2%)
  other arithmetic  12.3 us (2%)
    all_gather x3, blocking collectives, project(): lax.all_gather(partial_value, ('row', 'col'), axis=0, tiled=True)  327 us
    psum x1, blocking collectives, on_device(): energy = lax.psum(energy_local, ('row', 'col'))  79.8 us
    psum x1, blocking collectives, on_device(): lax.psum(jnp.sum(spread_dir * applied_dir, axis=1), ('row', 'col'))  76.4 us
    ppermute x20, waiting for transfers between devices, shifted(): return lax.ppermute(block, axis, route)  30.9 us
    ppermute x20, starting transfers between devices, shifted(): return lax.ppermute(block, axis, route)  26 us
    gather x7, local copies, waits for them, and re-layouts, jump_faces(): picked = jnp.take(vectors, face_where, axis=1)  22.6 us
    scatter x7, local copies, waits for them, and re-layouts, spread_faces(): jnp.zeros((values.shape[1], NB), jnp.float32).at[:, face_where].set(pieces)  18.4 us
  transfers between devices with their start and end apart: 20, of which 13 were waited for; matrix products, arithmetic and copies ran while one was open for 1% of the time, Pallas kernels for 0%

commit v1 on v0

--- a/solution.py
+++ b/solution.py
@@ -7,6 +7,10 @@
 highest = lax.Precision.HIGHEST
 contract_last = (((1,), (1,)), ((), ()))
 contract_first = (((0,), (0,)), ((), ()))
+open_face_in = lambda packet: jnp.concatenate(
+    lax.all_to_all(jnp.stack(lax.axis_size(("row", "col")) * [packet]), ("row", "col"), 0, 0),
+    axis=0,
+)
 
 
 def shifted(block, axis, distance):
@@ -35,11 +39,7 @@
 def project(values, face_where, rigid_local, coarse_rows):
     spread = spread_faces(values, face_where)
     partial_value = lax.dot_general(rigid_local, spread, contract_last, precision=highest)
-    coarse_coef = jnp.dot(
-        coarse_rows,
-        lax.all_gather(partial_value, ("row", "col"), axis=0, tiled=True),
-        precision=highest,
-    )
+    coarse_coef = jnp.dot(coarse_rows, open_face_in(partial_value), precision=highest)
     modes_back = lax.dot_general(coarse_coef, rigid_local, contract_first, precision=highest)
     correction = jump_faces(modes_back, face_where)
     return values - correction

time: 627 us -> 423 us (0.67)
  blocking collectives: 483 us -> 230 us
  waiting for transfers between devices: 30.9 us -> 60.1 us
  starting transfers between devices: 26 us -> 44 us
    all_gather x3 -> x0, blocking collectives: 327 us -> none  [project(): lax.all_gather(partial_value, ('row', 'col'), axis=0, tiled=True)]
    all_to_all x0 -> x2, blocking collectives: none -> 77.6 us  [lax.all_to_all(jnp.stack(lax.axis_size(('row', 'col')) * [packet]), ('row...]
    all_to_all x0 -> x1, waiting for transfers between devices: none -> 28.3 us  [lax.all_to_all(jnp.stack(lax.axis_size(('row', 'col')) * [packet]), ('row...]
    all_to_all x0 -> x1, starting transfers between devices: none -> 15.4 us  [lax.all_to_all(jnp.stack(lax.axis_size(('row', 'col')) * [packet]), ('row...]
  transfers between devices with their start and end apart: 20 -> 21, of which waited for: 13 -> 14; matrix products, arithmetic and copies ran while one was open for 1% -> 2% of each run, Pallas kernels for 0% -> 0%
where the time goes in v1:
time: 423 us; the launch traced here: 421 us
  blocking collectives  230 us (54%)
  waiting for transfers between devices  60.1 us (14%)
  local copies, waits for them, and re-layouts  59 us (14%)
  starting transfers between devices  44 us (10%)
  matrix products  14.4 us (3%)
  other arithmetic  12.3 us (3%)
    all_to_all x2, blocking collectives, lax.all_to_all(jnp.stack(lax.axis_size(('row', 'col')) * [packet]), ('row...  77.6 us
    psum x1, blocking collectives, on_device(): lax.psum(jnp.sum(spread_dir * applied_dir, axis=1), ('row', 'col'))  76.7 us
    psum x1, blocking collectives, on_device(): energy = lax.psum(energy_local, ('row', 'col'))  76.2 us
    ppermute x20, waiting for transfers between devices, shifted(): return lax.ppermute(block, axis, route)  31.8 us
    ppermute x20, starting transfers between devices, shifted(): return lax.ppermute(block, axis, route)  28.6 us
    all_to_all x1, waiting for transfers between devices, lax.all_to_all(jnp.stack(lax.axis_size(('row', 'col')) * [packet]), ('row...  28.3 us
    gather x7, local copies, waits for them, and re-layouts, jump_faces(): picked = jnp.take(vectors, face_where, axis=1)  22.5 us
    scatter x7, local copies, waits for them, and re-layouts, spread_faces(): jnp.zeros((values.shape[1], NB), jnp.float32).at[:, face_where].set(pieces)  18.4 us
  transfers between devices with their start and end apart: 21, of which 14 were waited for; matrix products, arithmetic and copies ran while one was open for 2% of the time, Pallas kernels for 0%

profile of v1, /device:TPU:1, one launch (start us, length us, event | category | flops | bytes accessed | tf_op | source)
XLA Modules:
  0.0 421.5 jit_solution(7339732432678487662)
XLA Ops:
  9.4 3.6 scatter_custom_fusion
  15.3 15.4 %all-to-all-start = ((f32[256,6,16]{2,1,0:T(8,128)}), f32[256,6,16]{2,1,0:T(8,128)}, u32[]{:S(2)}, u32[]{:S(2)}) async-start(f32[256,6,16]{2,1,0:T(8,128)} %stack.48), calls=%async_computation | async-start | bytes 2097152 | tf_op jit(solution)/shard_map/all_to_all | solution.py:11
  31.4 28.3 %all-to-all-done = f32[256,6,16]{2,1,0:T(8,128)} async-done(((f32[256,6,16]{2,1,0:T(8,128)}), f32[256,6,16]{2,1,0:T(8,128)}, u32[]{:S(2)}, u32[]{:S(2)}) %all-to-all-start) | async-done | bytes 98336 | tf_op jit(solution)/shard_map/all_to_all | solution.py:11
  62.6 4.0 gather_fusion
  67.9 2.7 collective-permute-start.2
  76.2 3.1 collective-permute-done.3
  81.4 4.7 %collective-permute-done.4 = f32[16,256]{1,0:T(8,128)S(1)} collective-permute-done((f32[16,256]{1,0:T(8,128)S(1)}, f32[16,256]{1,0:T(8,128)S(1)}, u32[]{:S(2)}, u32[]{:S(2)}) %collective-permute-start.4) | collective-permute-done | bytes 16416 | tf_op jit(solution)/shard_map/ppermute | solution.py:19
  87.2 3.6 scatter_custom_fusion.1
  98.1 4.0 gather_fusion.1
  106.0 3.3 collective-permute-start.7
  110.2 5.6 %collective-permute-done.8 = f32[16,256]{1,0:T(8,128)S(1)} collective-permute-done((f32[16,256]{1,0:T(8,128)S(1)}, f32[16,256]{1,0:T(8,128)S(1)}, u32[]{:S(2)}, u32[]{:S(2)}) %collective-permute-start.8) | collective-permute-done | bytes 16416 | tf_op jit(solution)/shard_map/ppermute | solution.py:19
  116.9 3.6 scatter_custom_fusion.2
  121.0 39.2 %all_to_all.15 = f32[256,6,16]{2,1,0:T(8,128)} all-to-all(f32[256,6,16]{2,1,0:T(8,128)S(1)} %stack.55), channel_id=1, replica_groups=mesh['row'=16,'col'=16] {'row','col'}, dimensions={0} | all-to-all | bytes 196608 | tf_op jit(solution)/shard_map/all_to_all | solution.py:11
  163.2 4.0 gather_fusion.2
  168.5 2.7 collective-permute-start.10
  178.6 76.2 %psum.14 = f32[16]{0:T(128)S(1)} all-reduce(f32[16]{0:T(128)} %get-tuple-element.37), channel_id=1, replica_groups=mesh['row'=16,'col'=16] {'row','col'}, use_global_device_ids=true, to_apply=%region_3.5 | all-reduce | flops 16 | bytes 128 | tf_op jit(solution)/shard_map/psum | solution.py:93
  257.1 3.6 scatter_custom_fusion.3
  264.2 4.0 gather_fusion.3
  276.0 3.8 collective-permute-done.16
  280.9 3.6 scatter_custom_fusion.4
  285.1 38.4 %all_to_all.16 = f32[256,6,16]{2,1,0:T(8,128)} all-to-all(f32[256,6,16]{2,1,0:T(8,128)S(1)} %stack.68), channel_id=1, replica_groups=mesh['row'=16,'col'=16] {'row','col'}, dimensions={0} | all-to-all | bytes 196608 | tf_op jit(solution)/shard_map/all_to_all | solution.py:11
  326.5 4.0 gather_fusion.4
  331.8 2.7 collective-permute-start.18
  341.6 76.7 %psum.15 = f32[16]{0:T(128)S(1)} all-reduce(f32[16]{0:T(128)} %get-tuple-element.12), channel_id=1, replica_groups=mesh['row'=16,'col'=16] {'row','col'}, use_global_device_ids=true, to_apply=%region_7.9 | all-reduce | flops 16 | bytes 128 | tf_op jit(solution)/shard_map/psum | solution.py:97
  (162 shorter events, 79.3 us)
Async XLA Ops:
  1.5 6.9 %collective-permute-start = (f32[16,256]{1,0:T(8,128)S(1)}, f32[16,256]{1,0:T(8,128)S(1)}, u32[]{:S(2)}, u32[]{:S(2)}) collective-permute-start(f32[16,256]{1,0:T(8,128)S(1)} %get-tuple-element.34), channel_id=1, source_target_pairs={{15,0},{0,1},{1,2},{2,3},{3,4},{4,5},{5,6},{6,7},{7,8},{8,9},{9,10... | collective-permute-start | bytes 49160 | tf_op jit(solution)/shard_map/ppermute | solution.py:19
  3.6 4.8 %collective-permute-start.1 = (f32[16,256]{1,0:T(8,128)S(1)}, f32[16,256]{1,0:T(8,128)S(1)}, u32[]{:S(2)}, u32[]{:S(2)}) collective-permute-start(f32[16,256]{1,0:T(8,128)S(1)} %get-tuple-element.35), channel_id=1, source_target_pairs={{240,0},{0,16},{16,32},{32,48},{48,64},{64,80},{80,96},{96,112},{1... | collective-permute-start | bytes 49160 | tf_op jit(solution)/shard_map/ppermute | solution.py:19
  15.3 44.3 %all-to-all-start = ((f32[256,6,16]{2,1,0:T(8,128)}), f32[256,6,16]{2,1,0:T(8,128)}, u32[]{:S(2)}, u32[]{:S(2)}) async-start(f32[256,6,16]{2,1,0:T(8,128)} %stack.48), calls=%async_computation | async-start | bytes 2097152 | tf_op jit(solution)/shard_map/all_to_all | solution.py:11
  67.9 5.0 %collective-permute-start.2 = (f32[16,256]{0,1:T(8,128)S(1)}, f32[16,256]{0,1:T(8,128)S(1)}, u32[]{:S(2)}, u32[]{:S(2)}) collective-permute-start(f32[16,256]{0,1:T(8,128)S(1)} %slice.139), channel_id=1, source_target_pairs={{1,0},{2,1},{3,2},{4,3},{5,4},{6,5},{7,6},{8,7},{9,8},{10,9},{11,1... | collective-permute-start | bytes 49160 | tf_op jit(solution)/shard_map/ppermute | solution.py:19
  73.6 5.6 %collective-permute-start.3 = (f32[16,256]{0,1:T(8,128)}, f32[16,256]{0,1:T(8,128)S(1)}, u32[]{:S(2)}, u32[]{:S(2)}) collective-permute-start(f32[16,256]{0,1:T(8,128)} %get-tuple-element.25), channel_id=1, source_target_pairs={{16,0},{32,16},{48,32},{64,48},{80,64},{96,80},{112,96},{128,112},... | collective-permute-start | bytes 49160 | tf_op jit(solution)/shard_map/ppermute | solution.py:19
  80.1 6.1 %collective-permute-start.4 = (f32[16,256]{1,0:T(8,128)S(1)}, f32[16,256]{1,0:T(8,128)S(1)}, u32[]{:S(2)}, u32[]{:S(2)}) collective-permute-start(f32[16,256]{1,0:T(8,128)S(1)} %get-tuple-element.32), channel_id=1, source_target_pairs={{15,0},{0,1},{1,2},{2,3},{3,4},{4,5},{5,6},{6,7},{7,8},{8,9},{9,10... | collective-permute-start | bytes 49160 | tf_op jit(solution)/shard_map/ppermute | solution.py:19
  81.2 5.0 %collective-permute-start.5 = (f32[16,256]{1,0:T(8,128)S(1)}, f32[16,256]{1,0:T(8,128)S(1)}, u32[]{:S(2)}, u32[]{:S(2)}) collective-permute-start(f32[16,256]{1,0:T(8,128)S(1)} %get-tuple-element.33), channel_id=1, source_target_pairs={{240,0},{0,16},{16,32},{32,48},{48,64},{64,80},{80,96},{96,112},{1... | collective-permute-start | bytes 49160 | tf_op jit(solution)/shard_map/ppermute | solution.py:19
  103.4 2.7 collective-permute-start.6
  106.0 4.2 collective-permute-start.7
  109.4 6.5 %collective-permute-start.8 = (f32[16,256]{1,0:T(8,128)S(1)}, f32[16,256]{1,0:T(8,128)S(1)}, u32[]{:S(2)}, u32[]{:S(2)}) collective-permute-start(f32[16,256]{1,0:T(8,128)S(1)} %get-tuple-element.30), channel_id=1, source_target_pairs={{15,0},{0,1},{1,2},{2,3},{3,4},{4,5},{5,6},{6,7},{7,8},{8,9},{9,10... | collective-permute-start | bytes 49160 | tf_op jit(solution)/shard_map/ppermute | solution.py:19
  110.2 5.6 %collective-permute-start.9 = (f32[16,256]{1,0:T(8,128)S(1)}, f32[16,256]{1,0:T(8,128)S(1)}, u32[]{:S(2)}, u32[]{:S(2)}) collective-permute-start(f32[16,256]{1,0:T(8,128)S(1)} %slice_subtract_fusion.8), channel_id=1, source_target_pairs={{240,0},{0,16},{16,32},{32,48},{48,64},{64,80},{80,96},{96,112},{1... | collective-permute-start | bytes 49160 | tf_op jit(solution)/shard_map/ppermute | solution.py:19
  168.5 5.0 %collective-permute-start.10 = (f32[16,256]{0,1:T(8,128)S(1)}, f32[16,256]{0,1:T(8,128)S(1)}, u32[]{:S(2)}, u32[]{:S(2)}) collective-permute-start(f32[16,256]{0,1:T(8,128)S(1)} %get-tuple-element.22), channel_id=1, source_target_pairs={{1,0},{2,1},{3,2},{4,3},{5,4},{6,5},{7,6},{8,7},{9,8},{10,9},{11,1... | collective-permute-start | bytes 49160 | tf_op jit(solution)/shard_map/ppermute | solution.py:19
  171.2 4.4 %collective-permute-start.11 = (f32[16,256]{0,1:T(8,128)S(1)}, f32[16,256]{0,1:T(8,128)S(1)}, u32[]{:S(2)}, u32[]{:S(2)}) collective-permute-start(f32[16,256]{0,1:T(8,128)S(1)} %get-tuple-element.23), channel_id=1, source_target_pairs={{16,0},{32,16},{48,32},{64,48},{80,64},{96,80},{112,96},{128,112},... | collective-permute-start | bytes 49160 | tf_op jit(solution)/shard_map/ppermute | solution.py:19
  176.5 79.5 %collective-permute-start.12 = (f32[32,256]{1,0:T(8,128)S(1)}, f32[32,256]{1,0:T(8,128)S(1)}, u32[]{:S(2)}, u32[]{:S(2)}) collective-permute-start(f32[32,256]{1,0:T(8,128)S(1)} %get-tuple-element.28), channel_id=1, source_target_pairs={{15,0},{0,1},{1,2},{2,3},{3,4},{4,5},{5,6},{6,7},{7,8},{8,9},{9,10... | collective-permute-start | bytes 98312 | tf_op jit(solution)/shard_map/ppermute | solution.py:19
  176.8 79.3 %collective-permute-start.13 = (f32[32,256]{1,0:T(8,128)S(1)}, f32[32,256]{1,0:T(8,128)S(1)}, u32[]{:S(2)}, u32[]{:S(2)}) collective-permute-start(f32[32,256]{1,0:T(8,128)S(1)} %get-tuple-element.29), channel_id=1, source_target_pairs={{240,0},{0,16},{16,32},{32,48},{48,64},{64,80},{80,96},{96,112},{1... | collective-permute-start | bytes 98312 | tf_op jit(solution)/shard_map/ppermute | solution.py:19
  269.5 2.7 collective-permute-start.14
  272.2 3.9 collective-permute-start.15
  274.0 5.9 %collective-permute-start.16 = (f32[16,256]{1,0:T(8,128)S(1)}, f32[16,256]{1,0:T(8,128)S(1)}, u32[]{:S(2)}, u32[]{:S(2)}) collective-permute-start(f32[16,256]{1,0:T(8,128)S(1)} %get-tuple-element.26), channel_id=1, source_target_pairs={{15,0},{0,1},{1,2},{2,3},{3,4},{4,5},{5,6},{6,7},{7,8},{8,9},{9,10... | collective-permute-start | bytes 49160 | tf_op jit(solution)/shard_map/ppermute | solution.py:19
  276.0 3.9 collective-permute-start.17
  325.3 94.6 %copy-start.8 = (f32[16,256]{1,0:T(8,128)S(1)}, f32[16,256]{1,0:T(8,128)}, u32[]{:S(2)}) copy-start(f32[16,256]{1,0:T(8,128)} %copy-done.6) | copy-start | bytes 49156
  325.3 94.6 %copy-start.11 = (f32[16,256]{1,0:T(8,128)S(1)}, f32[16,256]{1,0:T(8,128)}, u32[]{:S(2)}) copy-start(f32[16,256]{1,0:T(8,128)} %copy-done.9) | copy-start | bytes 49156
  325.3 94.6 %copy-start.13 = (f32[16,256]{1,0:T(8,128)S(1)}, f32[16,256]{1,0:T(8,128)}, u32[]{:S(2)}) copy-start(f32[16,256]{1,0:T(8,128)} %copy-done.12) | copy-start | bytes 49156
  331.8 5.0 %collective-permute-start.18 = (f32[16,256]{0,1:T(8,128)S(1)}, f32[16,256]{0,1:T(8,128)S(1)}, u32[]{:S(2)}, u32[]{:S(2)}) collective-permute-start(f32[16,256]{0,1:T(8,128)S(1)} %slice.163), channel_id=1, source_target_pairs={{1,0},{2,1},{3,2},{4,3},{5,4},{6,5},{7,6},{8,7},{9,8},{10,9},{11,1... | collective-permute-start | bytes 49160 | tf_op jit(solution)/shard_map/ppermute | solution.py:19
  337.5 81.5 %collective-permute-start.19 = (f32[16,256]{0,1:T(8,128)}, f32[16,256]{0,1:T(8,128)}, u32[]{:S(2)}, u32[]{:S(2)}) collective-permute-start(f32[16,256]{0,1:T(8,128)} %get-tuple-element.19), channel_id=1, source_target_pairs={{16,0},{32,16},{48,32},{64,48},{80,64},{96,80},{112,96},{128,112},... | collective-permute-start | bytes 49160 | tf_op jit(solution)/shard_map/ppermute | solution.py:19
  (19 other events, 462.8 us)
